TPU v7x, 512 devices: a whole 4x4x16 slice. The times are simulated.
512 devices in a mesh: seq: 64 (over z, y_lo, core), head: 8 (over x, y_hi).
Axes of the slice: x: 4, y: 4 (y_hi: 2, y_lo: 2; y = y_hi * 2 + y_lo), z: 16, core: 2. Of those that a mesh axis runs over, the one named last changes fastest.
Arguments:
- queries: bfloat16 [4096, 3072], P('seq', 'head'), may hold values from -10 to 10
- suffix_latent: bfloat16 [4096, 576], P('seq'), may hold values from -6 to 6
- prefix_latent: bfloat16 [1024, 576], P('seq'), may hold values from -6 to 6
- kv_up: bfloat16 [16, 512, 256], P('head'), may hold values from -0.25 to 0.25
- w_out: bfloat16 [2048, 2048], P('head'), may hold values from -2 to 2
- residual: bfloat16 [4096, 2048], P('seq'), may hold values from -400 to 400
- norm_gain: bfloat16 [2048], replicated, may hold values from 0.099609375 to 1.8984375
- router: bfloat16 [2048, 64], replicated, may hold values from -0.125 to 0.125
- w_gate: bfloat16 [64, 2048, 1408], P('seq', None, 'head'), may hold values from -0.125 to 0.125
- w_up: bfloat16 [64, 2048, 1408], P('seq', None, 'head'), may hold values from -0.125 to 0.125
- w_down: bfloat16 [64, 1408, 2048], P('seq', 'head'), may hold values from -0.15625 to 0.15625
- lengths: int32 [128], replicated, may hold values from 1 to 64, 4096 in all
- group_map: int32 [128], replicated, may hold values from 0 to 1
- expert_ids: int32 [4096, 6], P('seq'), may hold values from 0 to 63, all different within a row; in each aligned block of 64 rows (0 to 63, 64 to 127, ...) at most 9 rows name the same one
Outputs:
- attention: bfloat16 [4096, 2048], P('seq', 'head')
- expert_out: bfloat16 [4096, 2048], P('seq', 'head')
Inputs may be any that keep to these rules, and one draw needn't show every extreme that they name: `lengths`: the requests cover the 4096 tokens exactly; each has 1 to 64 tokens, and one has exactly 64. `expert_ids`: each token names 6 different experts. Among the 64 tokens of one index of seq (aligned blocks of rows) no expert is named more than 9 times, a bound that some block reaches.
All inputs are finite; a program needn't handle non-finite values.
Results may differ from a plain program's by a relative error of at most 0.027.
Values may be sent and summed in bfloat16 or wider, within the bound.
A program may use at most 64 MiB of HBM per device.

v0:
```python
import math
import jax
import jax.numpy as jnp
from jax import lax
from jax.sharding import PartitionSpec as P

D = 2048
NOPE = 128
ROPE = 64
VDIM = 128
LAT = 512
TOPK = 6
PRE_LEN = 512
score_scale = 1.0 / math.sqrt(192.0)
route_scale = 2.446
norm_eps = 1e-06


def shifted(value, axis, by):
    peers = lax.axis_size(axis)
    pairs = [(i, i + by) for i in range(peers) if 0 <= i + by < peers]
    return lax.ppermute(value, axis, pairs)


def request_info(lengths, group_map, position):
    request_ends = jnp.cumsum(lengths)
    request_starts = request_ends - lengths
    request_index = jnp.sum((request_ends[None, :] <= position[:, None]).astype(jnp.int32), axis=1)
    member = (
        request_index[:, None] == jnp.arange(lengths.shape[0], dtype=jnp.int32)[None, :]
    ).astype(jnp.int32)
    first_token = jnp.sum(member * request_starts[None, :], axis=1)
    token_group = jnp.sum(member * group_map[None, :], axis=1)
    return (first_token, token_group)


def on_device(
    queries,
    suffix_latent,
    prefix_latent,
    kv_up,
    w_out,
    residual,
    norm_gain,
    router,
    w_gate,
    w_up,
    w_down,
    lengths,
    group_map,
    expert_ids,
):
    tok_count = queries.shape[0]
    head_local = kv_up.shape[0]
    seq_index = lax.axis_index("seq")
    first_row = seq_index * tok_count
    position = first_row + jnp.arange(tok_count, dtype=jnp.int32)
    first_token, token_group = request_info(lengths, group_map, position)
    query_block = queries.reshape(tok_count, head_local, NOPE + ROPE)
    absorbed = jnp.einsum(
        "thn,hln->thl",
        query_block[:, :, :NOPE],
        kv_up[:, :, :NOPE],
        preferred_element_type=jnp.float32,
    ).astype(jnp.bfloat16)
    joined = jnp.concatenate([absorbed, query_block[:, :, NOPE:]], axis=2).reshape(
        tok_count * head_local, LAT + ROPE
    )
    earlier = shifted(suffix_latent, "seq", 1)
    nearby = jnp.concatenate([earlier, suffix_latent], axis=0)
    near_pos = first_row - tok_count + jnp.arange(2 * tok_count, dtype=jnp.int32)
    near_seen = (near_pos[None, :] >= first_token[:, None]) & (
        near_pos[None, :] <= position[:, None]
    )
    near_seen = jnp.repeat(near_seen, head_local, axis=0)
    scores = jnp.dot(joined, nearby.T, preferred_element_type=jnp.float32) * score_scale
    row_max = jnp.max(jnp.where(near_seen, scores, -jnp.inf), axis=1, keepdims=True)
    weights = jnp.where(near_seen, jnp.exp(scores - row_max), 0.0)
    total = jnp.sum(weights, axis=1, keepdims=True)
    weighted = jnp.dot(
        weights.astype(jnp.bfloat16), nearby[:, :LAT], preferred_element_type=jnp.float32
    )
    group_rows = jnp.repeat(token_group, head_local)
    piece = lax.all_gather(prefix_latent, "seq", axis=0, tiled=True)
    row_group = jnp.arange(piece.shape[0], dtype=jnp.int32) // PRE_LEN
    visible = row_group[None, :] == group_rows[:, None]
    piece_scores = jnp.dot(joined, piece.T, preferred_element_type=jnp.float32) * score_scale
    new_max = jnp.maximum(
        row_max, jnp.max(jnp.where(visible, piece_scores, -jnp.inf), axis=1, keepdims=True)
    )
    piece_weights = jnp.where(visible, jnp.exp(piece_scores - new_max), 0.0)
    factor = jnp.exp(row_max - new_max)
    new_total = total * factor + jnp.sum(piece_weights, axis=1, keepdims=True)
    new_weighted = weighted * factor + jnp.dot(
        piece_weights.astype(jnp.bfloat16), piece[:, :LAT], preferred_element_type=jnp.float32
    )
    mixed = (new_weighted / new_total).astype(jnp.bfloat16).reshape(tok_count, head_local, LAT)
    heads_out = jnp.einsum(
        "thl,hlv->thv", mixed, kv_up[:, :, NOPE:], preferred_element_type=jnp.float32
    ).astype(jnp.bfloat16)
    partial_value = jnp.dot(
        heads_out.reshape(tok_count, head_local * VDIM), w_out, preferred_element_type=jnp.float32
    )
    col_width = D // lax.axis_size("head")
    col_start = lax.axis_index("head") * col_width
    attention_sum = lax.psum(partial_value.astype(jnp.bfloat16), "head").astype(jnp.float32)
    attention = lax.dynamic_slice_in_dim(attention_sum, col_start, col_width, 1).astype(
        jnp.bfloat16
    )
    hidden_state = residual.astype(jnp.float32) + attention_sum
    mean_square = jnp.mean(hidden_state * hidden_state, axis=1, keepdims=True)
    normed = (
        hidden_state * lax.rsqrt(mean_square + norm_eps) * norm_gain.astype(jnp.float32)
    ).astype(jnp.bfloat16)
    logits = jnp.dot(normed, router, preferred_element_type=jnp.float32)
    expert_count = router.shape[1]
    capacity = (3 * tok_count * TOPK + 2 * expert_count - 1) // (2 * expert_count)
    member = expert_ids[:, :, None] == jnp.arange(expert_count, dtype=jnp.int32)[None, None, :]
    chosen = jnp.sum(jnp.where(member, jax.nn.sigmoid(logits)[:, None, :], 0.0), axis=2)
    gates = chosen / jnp.sum(chosen, axis=1, keepdims=True) * route_scale
    flat_member = member.reshape(tok_count * TOPK, expert_count).astype(jnp.int32)
    running = jnp.cumsum(flat_member, axis=0)
    slot_rank = jnp.sum(flat_member * running, axis=1) - 1
    slot_index = expert_ids.reshape(-1) * capacity + slot_rank
    pair_token = jnp.arange(tok_count * TOPK, dtype=jnp.int32) // TOPK
    source_row = jnp.zeros((expert_count * capacity,), jnp.int32).at[slot_index].set(pair_token + 1)
    padded_rows = jnp.concatenate([jnp.zeros((1, normed.shape[1]), jnp.bfloat16), normed], axis=0)
    outgoing = padded_rows[source_row].reshape(expert_count, capacity, normed.shape[1])
    local_experts = w_gate.shape[0]
    received = lax.all_to_all(outgoing, "seq", split_axis=0, concat_axis=0, tiled=True)
    shaped = received.reshape(-1, local_experts, received.shape[1], received.shape[2])
    gate_part = jnp.einsum("secd,edf->secf", shaped, w_gate, preferred_element_type=jnp.float32)
    up_part = jnp.einsum("secd,edf->secf", shaped, w_up, preferred_element_type=jnp.float32)
    inner = (jax.nn.silu(gate_part) * up_part).astype(jnp.bfloat16)
    down_part = jnp.einsum(
        "secf,efd->secd", inner, w_down, preferred_element_type=jnp.float32
    ).astype(jnp.bfloat16)
    produced = down_part.reshape(-1, down_part.shape[2], down_part.shape[3])
    returned = lax.all_to_all(produced, "seq", split_axis=0, concat_axis=0, tiled=True)
    picked = returned.reshape(expert_count * capacity, returned.shape[2])[slot_index].reshape(
        tok_count, TOPK, returned.shape[2]
    )
    combined = jnp.sum(picked.astype(jnp.float32) * gates[:, :, None], axis=1)
    expert_out = lax.psum_scatter(
        combined.astype(jnp.bfloat16), "head", scatter_dimension=1, tiled=True
    )
    return (attention, expert_out)


def solution(mesh):
    placed = (
        P("seq", "head"),
        P("seq", None),
        P("seq", None),
        P("head", None, None),
        P("head", None),
        P("seq", None),
        P(),
        P(),
        P("seq", None, "head"),
        P("seq", None, "head"),
        P("seq", "head", None),
        P(),
        P(),
        P("seq", None),
    )
    return jax.shard_map(
        on_device,
        mesh=mesh,
        in_specs=placed,
        out_specs=(P("seq", "head"), P("seq", "head")),
        check_vma=False,
    )
```

profile of v0, /device:TPU:2, one launch (start us, length us, event | category | flops | bytes accessed | tf_op | source)
XLA Modules:
  0.0 760.6 jit_solution(14834072606422764430)
XLA Ops:
  7.2 0.7 all-gather.2.cloned.1.call-update
  8.0 1.7 collective-permute-start
  9.7 0.7 broadcast_multiply_fusion
  10.4 0.8 copy.50
  11.2 0.2 reduce-window.18
  11.5 0.2 convert_reduce_fusion
  11.7 0.8 copy.59
  12.6 0.1 eq.67
  12.7 0.9 reshape.210
  13.7 0.7 sub.51
  14.4 0.7 convert_element_type.78
  15.1 0.1 mul.133
  15.3 0.8 select_reduce_fusion.3
  16.5 0.1 eq.64
  16.7 0.9 reduce-window.19
  17.6 0.2 slice_reduce_fusion
  17.9 1.2 fusion.10
  19.0 0.2 copy.53
  19.5 2.9 scatter_custom_fusion
  22.5 0.2 select_reduce_fusion.2
  22.8 113.3 %all-gather.2.cloned.1.call-done = bf16[1024,576]{1,0:T(8,128)(2,1)} async-done(((bf16[16,576]{1,0:T(8,128)(2,1)}), bf16[1024,576]{1,0:T(8,128)(2,1)}) %all-gather.2.cloned.1.call-update) | async-done | bytes 1179664 | tf_op jit(solution)/shard_map/all_gather | solution.py:84
  136.1 2.1 fusion.26
  138.2 0.3 fusion.27
  138.5 0.4 fusion.15
  138.8 0.2 fusion.7
  139.2 0.2 fusion.11
  139.4 1.0 convolution_convert_fusion.1
  140.4 95.5 %all-reduce.3.cloned.1.call-done = bf16[64,2048]{1,0:T(8,128)(2,1)} async-done(((bf16[64,2048]{1,0:T(8,128)(2,1)}), bf16[64,2048]{1,0:T(8,128)(2,1)}) %all-reduce.3.cloned.1.call-update) | async-done | bytes 262160 | tf_op jit(solution)/shard_map/psum | solution.py:106
  235.9 1.1 multiply_reduce_fusion.1
  237.1 1.1 multiply_convert_fusion
  238.1 0.7 copy-done.4
  238.9 4.0 gather_fusion
  242.9 4.6 reshape.215
  247.5 204.3 %all_to_all.10 = bf16[64,9,2048]{2,1,0:T(8,128)(2,1)S(1)} all-to-all(bf16[64,9,2048]{2,1,0:T(8,128)(2,1)} %reshape.215), channel_id=1, replica_groups=mesh['seq'=64,'head'=8] {'seq'}, dimensions={0} | all-to-all | bytes 4718592 | tf_op jit(solution)/shard_map/all_to_all | solution.py:130
  451.8 1.9 copy-done.1
  453.7 3.5 convolution_bitcast_fusion.1
  457.2 5.6 convolution_convert_fusion
  462.8 3.5 copy.64
  466.3 5.8 all-to-all-start.1
  472.2 0.2 fusion.14
  472.4 0.3 select_reduce_fusion
  472.8 190.1 %all-to-all-done.1 = bf16[64,9,2048]{2,1,0:T(8,128)(2,1)} async-done(((bf16[64,9,2048]{2,1,0:T(8,128)(2,1)}), bf16[64,9,2048]{2,1,0:T(8,128)(2,1)}, u32[]{:S(2)}, u32[]{:S(2)}) %all-to-all-start.1) | async-done | bytes 2359328 | tf_op jit(solution)/shard_map/all_to_all | solution.py:139
  662.9 3.4 reshape.220
  666.3 3.1 gather_fusion.1
  669.4 3.9 reshape.221
  673.3 4.5 multiply_reduce_fusion
  677.8 1.4 dynamic-slice_convert_fusion
  679.1 74.9 %reduce-scatter.2.cloned.1.call-done = bf16[64,256]{1,0:T(8,128)(2,1)} async-done(((bf16[64,2048]{1,0:T(8,128)(2,1)}), bf16[64,256]{1,0:T(8,128)(2,1)}) %reduce-scatter.2.cloned.1.call-update) | async-done | bytes 32784 | tf_op jit(solution)/shard_map/reduce_scatter | solution.py:144
  (61 shorter events, 1.7 us)
Async XLA Ops:
  7.2 132.2 %copy-start = (bf16[256,2048]{1,0:T(8,128)(2,1)S(1)}, bf16[256,2048]{1,0:T(8,128)(2,1)}, u32[]{:S(2)}) copy-start(bf16[256,2048]{1,0:T(8,128)(2,1)} %param.18) | copy-start | bytes 3145732
  7.2 15.3 %copy-start.7 = (bf16[64,576]{1,0:T(8,128)(2,1)S(1)}, bf16[64,576]{1,0:T(8,128)(2,1)}, u32[]{:S(2)}) copy-start(bf16[64,576]{1,0:T(8,128)(2,1)} %param.15) | copy-start | bytes 221188
  7.2 128.9 %all-gather.2.cloned.1.call-start = ((), (), s32[]{:S(2)}) async-start(), calls=%async_computation.3 | async-start | bytes 1331200 | tf_op jit(solution)/shard_map/all_gather | solution.py:84
  7.9 228.0 %all-reduce.3.cloned.1.call-start = ((), (), s32[]{:S(2)}) async-start(), calls=%async_computation.4 | async-start | bytes 524288 | tf_op jit(solution)/shard_map/psum | solution.py:106
  8.0 14.5 %collective-permute-start = (bf16[64,576]{1,0:T(8,128)(2,1)}, bf16[64,576]{1,0:T(8,128)(2,1)S(1)}, u32[]{:S(2)}, u32[]{:S(2)}) collective-permute-start(bf16[64,576]{1,0:T(8,128)(2,1)} %param.15), channel_id=1, source_target_pairs={{0,8},{8,16},{16,24},{24,32},{32,40},{40,48},{48,56},{56,64},{64,7... | collective-permute-start | bytes 221192 | tf_op jit(solution)/shard_map/ppermute | solution.py:22
  136.1 2.4 copy-start.2
  138.2 1.0 copy-start.6
  138.5 97.5 %copy-start.3 = (bf16[64,2048]{1,0:T(8,128)(2,1)S(1)}, bf16[64,2048]{1,0:T(8,128)(2,1)}, u32[]{:S(2)}) copy-start(bf16[64,2048]{1,0:T(8,128)(2,1)} %param.19) | copy-start | bytes 786436
  238.1 0.7 copy-start.4
  247.5 206.2 %copy-start.9 = (bf16[1,2048,176]{1,2,0:T(8,128)(2,1)S(1)}, bf16[1,2048,176]{1,2,0:T(8,128)(2,1)}, u32[]{:S(2)}) copy-start(bf16[1,2048,176]{1,2,0:T(8,128)(2,1)} %param.22) | copy-start | bytes 2162692
  451.8 1.9 copy-start.1
  466.3 5.9 copy-start.5
  466.3 5.9 copy-start.10
  466.3 6.1 copy-start.8
  466.3 196.6 %all-to-all-start.1 = ((bf16[64,9,2048]{2,1,0:T(8,128)(2,1)}), bf16[64,9,2048]{2,1,0:T(8,128)(2,1)}, u32[]{:S(2)}, u32[]{:S(2)}) async-start(bf16[64,9,2048]{2,1,0:T(8,128)(2,1)} %copy.64), calls=%async_computation.1 | async-start | bytes 8388608 | tf_op jit(solution)/shard_map/all_to_all | solution.py:139
  472.1 282.0 %reduce-scatter.2.cloned.1.call-start = ((), (), s32[]{:S(2)}) async-start(), calls=%async_computation.5 | async-start | bytes 294912 | tf_op jit(solution)/shard_map/reduce_scatter | solution.py:144
Sparse Core Ops, SparseCore 0:
  10.1 125.8 all-gather.1
  140.5 95.3 all-reduce.2
  677.9 76.1 reduce-scatter.1
where the time goes:
time: 762 us; the launch traced here: 761 us
  waiting for transfers between devices  475 us (62%)
  blocking collectives  204 us (27%)
  local copies, waits for them, and re-layouts  33.7 us (4%)
  matrix products  14.5 us (2%)
  between operations  14.2 us (2%)
  other arithmetic  11.8 us (2%)
  starting transfers between devices  7.65 us (1%)
    all_to_all x1, blocking collectives, on_device(): lax.all_to_all(outgoing, 'seq', split_axis=0, concat_axis=0, tiled=True)  204 us
    all_to_all x1, waiting for transfers between devices, on_device(): lax.all_to_all(produced, 'seq', split_axis=0, concat_axis=0, tiled=True)  190 us
    all_gather x1, waiting for transfers between devices, on_device(): piece = lax.all_gather(prefix_latent, 'seq', axis=0, tiled=True)  113 us
    psum x1, waiting for transfers between devices, on_device(): lax.psum(partial_value.astype(jnp.bfloat16), 'head').astype(jnp.float32)  95.5 us
    reduce_scatter x1, waiting for transfers between devices, on_device(): lax.psum_scatter(combined.astype(jnp.bfloat16), 'head', scatter_dimension...  74.9 us
  transfers between devices with their start and end apart: 5, of which 4 were waited for; matrix products, arithmetic and copies ran while one was open for 2% of the time, Pallas kernels for 0%

commit v1 on v0

--- a/solution.py
+++ b/solution.py
@@ -81,7 +81,9 @@
         weights.astype(jnp.bfloat16), nearby[:, :LAT], preferred_element_type=jnp.float32
     )
     group_rows = jnp.repeat(token_group, head_local)
-    piece = lax.all_gather(prefix_latent, "seq", axis=0, tiled=True)
+    piece = jnp.concatenate(
+        lax.all_to_all(jnp.stack([prefix_latent] * lax.axis_size("seq")), "seq", 0, 0), axis=0
+    )
     row_group = jnp.arange(piece.shape[0], dtype=jnp.int32) // PRE_LEN
     visible = row_group[None, :] == group_rows[:, None]
     piece_scores = jnp.dot(joined, piece.T, preferred_element_type=jnp.float32) * score_scale

time: 762 us -> 714 us (0.937)
  waiting for transfers between devices: 475 us -> 415 us
  starting transfers between devices: 7.65 us -> 24.9 us
    all_gather x1 -> x0, waiting for transfers between devices: 113 us -> none  [on_device(): piece = lax.all_gather(prefix_latent, 'seq', axis=0, tiled=True)]
    all_to_all x0 -> x1, waiting for transfers between devices: none -> 58 us  [on_device(): lax.all_to_all(jnp.stack([prefix_latent] * lax.axis_size('seq')), 'seq',...]
    all_to_all x0 -> x1, starting transfers between devices: none -> 17.1 us  [on_device(): lax.all_to_all(jnp.stack([prefix_latent] * lax.axis_size('seq')), 'seq',...]
  transfers between devices with their start and end apart: 5 -> 5, of which waited for: 4 -> 4; matrix products, arithmetic and copies ran while one was open for 2% -> 1% of each run, Pallas kernels for 0% -> 0%
where the time goes in v1:
time: 714 us
  waiting for transfers between devices  415 us (58%)
  blocking collectives  204 us (29%)
  local copies, waits for them, and re-layouts  33.5 us (5%)
  starting transfers between devices  24.9 us (3%)
  between operations  14.6 us (2%)
  matrix products  12.1 us (2%)
  other arithmetic  9.12 us (1%)
    all_to_all x1, blocking collectives, on_device(): lax.all_to_all(outgoing, 'seq', split_axis=0, concat_axis=0, tiled=True)  204 us
    all_to_all x1, waiting for transfers between devices, on_device(): lax.all_to_all(produced, 'seq', split_axis=0, concat_axis=0, tiled=True)  190 us
    psum x1, waiting for transfers between devices, on_device(): lax.psum(partial_value.astype(jnp.bfloat16), 'head').astype(jnp.float32)  92 us
    reduce_scatter x1, waiting for transfers between devices, on_device(): lax.psum_scatter(combined.astype(jnp.bfloat16), 'head', scatter_dimension...  75 us
    all_to_all x1, waiting for transfers between devices, on_device(): lax.all_to_all(jnp.stack([prefix_latent] * lax.axis_size('seq')), 'seq',...  58 us
    all_to_all x1, starting transfers between devices, on_device(): lax.all_to_all(jnp.stack([prefix_latent] * lax.axis_size('seq')), 'seq',...  17.1 us
  transfers between devices with their start and end apart: 5, of which 4 were waited for; matrix products, arithmetic and copies ran while one was open for 1% of the time, Pallas kernels for 0%

profile of v1, /device:TPU:2, one launch (start us, length us, event | category | flops | bytes accessed | tf_op | source)
XLA Modules:
  0.0 713.6 jit_solution(13920339339650264264)
XLA Ops:
  7.3 2.0 stack.2
  9.3 17.1 %all-to-all-start = ((bf16[64,16,576]{2,1,0:T(8,128)(2,1)}), bf16[64,16,576]{2,1,0:T(8,128)(2,1)S(1)}, u32[]{:S(2)}, u32[]{:S(2)}) async-start(bf16[64,16,576]{2,1,0:T(8,128)(2,1)} %stack.2), calls=%async_computation | async-start | bytes 2621440 | tf_op jit(solution)/shard_map/all_to_all | solution.py:85
  26.4 2.0 collective-permute-start
  28.5 0.1 eq.71
  28.7 0.1 eq.67
  29.1 0.1 mul.133
  29.3 0.1 copy.50
  29.4 0.2 reduce-window.18
  29.6 0.1 reduce.1
  29.7 0.2 convert_reduce_fusion
  29.9 0.2 select_reduce_fusion.3
  30.3 0.1 copy.55
  30.4 0.1 eq.64
  30.6 0.9 reduce-window.19
  31.5 0.2 slice_reduce_fusion
  31.8 0.2 fusion.10
  32.0 0.2 copy.53
  32.2 0.1 reshape.216
  32.5 2.9 scatter_custom_fusion
  35.5 0.2 select_reduce_fusion.2
  35.8 58.0 %all-to-all-done = bf16[64,16,576]{2,1,0:T(8,128)(2,1)S(1)} async-done(((bf16[64,16,576]{2,1,0:T(8,128)(2,1)}), bf16[64,16,576]{2,1,0:T(8,128)(2,1)S(1)}, u32[]{:S(2)}, u32[]{:S(2)}) %all-to-all-start) | async-done | bytes 1179680 | tf_op jit(solution)/shard_map/all_to_all | solution.py:85
  93.7 0.6 fusion.26
  94.4 0.4 fusion.15
  94.8 0.3 fusion.27
  95.1 0.2 fusion.7
  95.4 0.2 fusion.11
  95.5 1.0 convolution_convert_fusion.1
  96.6 92.0 %all-reduce.3.cloned.1.call-done = bf16[64,2048]{1,0:T(8,128)(2,1)} async-done(((bf16[64,2048]{1,0:T(8,128)(2,1)}), bf16[64,2048]{1,0:T(8,128)(2,1)}) %all-reduce.3.cloned.1.call-update) | async-done | bytes 262160 | tf_op jit(solution)/shard_map/psum | solution.py:108
  188.5 1.1 multiply_reduce_fusion.1
  189.7 1.1 multiply_convert_fusion
  190.8 0.7 copy-done.3
  191.6 4.0 gather_fusion
  195.5 4.6 reshape.221
  200.1 204.3 %all_to_all.15 = bf16[64,9,2048]{2,1,0:T(8,128)(2,1)S(1)} all-to-all(bf16[64,9,2048]{2,1,0:T(8,128)(2,1)} %reshape.221), channel_id=1, replica_groups=mesh['seq'=64,'head'=8] {'seq'}, dimensions={0} | all-to-all | bytes 4718592 | tf_op jit(solution)/shard_map/all_to_all | solution.py:132
  404.5 1.9 copy-done.1
  406.4 3.5 convolution_bitcast_fusion.1
  409.9 5.6 convolution_convert_fusion
  415.4 3.5 copy.64
  418.9 5.8 all-to-all-start.2
  424.8 0.2 fusion.14
  425.0 0.3 select_reduce_fusion
  425.4 190.1 %all-to-all-done.2 = bf16[64,9,2048]{2,1,0:T(8,128)(2,1)} async-done(((bf16[64,9,2048]{2,1,0:T(8,128)(2,1)}), bf16[64,9,2048]{2,1,0:T(8,128)(2,1)}, u32[]{:S(2)}, u32[]{:S(2)}) %all-to-all-start.2) | async-done | bytes 2359328 | tf_op jit(solution)/shard_map/all_to_all | solution.py:141
  615.5 3.4 reshape.226
  618.9 3.1 gather_fusion.1
  622.0 3.9 reshape.227
  625.9 4.5 multiply_reduce_fusion
  630.4 1.4 dynamic-slice_convert_fusion
  631.8 75.0 %reduce-scatter.2.cloned.1.call-done = bf16[64,256]{1,0:T(8,128)(2,1)} async-done(((bf16[64,2048]{1,0:T(8,128)(2,1)}), bf16[64,256]{1,0:T(8,128)(2,1)}) %reduce-scatter.2.cloned.1.call-update) | async-done | bytes 32784 | tf_op jit(solution)/shard_map/reduce_scatter | solution.py:146
  (67 shorter events, 1.3 us)
Async XLA Ops:
  7.2 88.4 %copy-start = (bf16[256,2048]{1,0:T(8,128)(2,1)S(1)}, bf16[256,2048]{1,0:T(8,128)(2,1)}, u32[]{:S(2)}) copy-start(bf16[256,2048]{1,0:T(8,128)(2,1)} %param.18) | copy-start | bytes 3145732
  7.2 19.2 %copy-start.6 = (bf16[64,576]{1,0:T(8,128)(2,1)S(1)}, bf16[64,576]{1,0:T(8,128)(2,1)}, u32[]{:S(2)}) copy-start(bf16[64,576]{1,0:T(8,128)(2,1)} %param.15) | copy-start | bytes 221188
  7.2 21.2 %copy-start.8 = (s32[64,6]{0,1:T(8,128)S(1)}, s32[64,6]{0,1:T(8,128)}, u32[]{:S(2)}) copy-start(s32[64,6]{0,1:T(8,128)} %param.27) | copy-start | bytes 4612
  7.2 21.6 %copy-start.7 = (bf16[64,384]{1,0:T(8,128)(2,1)S(1)}, bf16[64,384]{1,0:T(8,128)(2,1)}, u32[]{:S(2)}) copy-start(bf16[64,384]{1,0:T(8,128)(2,1)} %param.14) | copy-start | bytes 147460
  7.2 21.8 %copy-start.9 = (bf16[2048]{0:T(1024)(128)(2,1)S(1)}, bf16[2048]{0:T(1024)(128)(2,1)}, u32[]{:S(2)}) copy-start(bf16[2048]{0:T(1024)(128)(2,1)} %param.20) | copy-start | bytes 12292
  7.2 22.0 %copy-start.10 = (s32[128]{0:T(128)S(1)}, s32[128]{0:T(128)}, u32[]{:S(2)}) copy-start(s32[128]{0:T(128)} %param.25) | copy-start | bytes 1540
  7.2 22.7 %copy-start.11 = (s32[128]{0:T(128)S(1)}, s32[128]{0:T(128)}, u32[]{:S(2)}) copy-start(s32[128]{0:T(128)} %param.26) | copy-start | bytes 1540
  7.2 24.5 %copy-start.5 = (bf16[2,512,256]{2,1,0:T(8,128)(2,1)S(1)}, bf16[2,512,256]{2,1,0:T(8,128)(2,1)}, u32[]{:S(2)}) copy-start(bf16[2,512,256]{2,1,0:T(8,128)(2,1)} %param.17) | copy-start | bytes 1572868
  9.3 84.5 %all-to-all-start = ((bf16[64,16,576]{2,1,0:T(8,128)(2,1)}), bf16[64,16,576]{2,1,0:T(8,128)(2,1)S(1)}, u32[]{:S(2)}, u32[]{:S(2)}) async-start(bf16[64,16,576]{2,1,0:T(8,128)(2,1)} %stack.2), calls=%async_computation | async-start | bytes 2621440 | tf_op jit(solution)/shard_map/all_to_all | solution.py:85
  26.4 162.2 %all-reduce.3.cloned.1.call-start = ((), (), s32[]{:S(2)}) async-start(), calls=%async_computation.4 | async-start | bytes 524288 | tf_op jit(solution)/shard_map/psum | solution.py:108
  26.4 9.0 %collective-permute-start = (bf16[64,576]{1,0:T(8,128)(2,1)S(1)}, bf16[64,576]{1,0:T(8,128)(2,1)S(1)}, u32[]{:S(2)}, u32[]{:S(2)}) collective-permute-start(bf16[64,576]{1,0:T(8,128)(2,1)S(1)} %copy-done.6), channel_id=1, source_target_pairs={{0,8},{8,16},{16,24},{24,32},{32,40},{40,48},{48,56},{56,64},{64,7... | collective-permute-start | bytes 221192 | tf_op jit(solution)/shard_map/ppermute | solution.py:22
  94.8 93.8 %copy-start.2 = (bf16[64,2048]{1,0:T(8,128)(2,1)S(1)}, bf16[64,2048]{1,0:T(8,128)(2,1)}, u32[]{:S(2)}) copy-start(bf16[64,2048]{1,0:T(8,128)(2,1)} %param.19) | copy-start | bytes 786436
  190.8 0.7 copy-start.3
  200.1 206.2 %copy-start.12 = (bf16[1,2048,176]{1,2,0:T(8,128)(2,1)S(1)}, bf16[1,2048,176]{1,2,0:T(8,128)(2,1)}, u32[]{:S(2)}) copy-start(bf16[1,2048,176]{1,2,0:T(8,128)(2,1)} %param.22) | copy-start | bytes 2162692
  404.5 1.9 copy-start.1
  418.9 5.9 copy-start.4
  418.9 5.9 copy-start.13
  418.9 196.6 %all-to-all-start.2 = ((bf16[64,9,2048]{2,1,0:T(8,128)(2,1)}), bf16[64,9,2048]{2,1,0:T(8,128)(2,1)}, u32[]{:S(2)}, u32[]{:S(2)}) async-start(bf16[64,9,2048]{2,1,0:T(8,128)(2,1)} %copy.64), calls=%async_computation.2 | async-start | bytes 8388608 | tf_op jit(solution)/shard_map/all_to_all | solution.py:141
  424.7 282.0 %reduce-scatter.2.cloned.1.call-start = ((), (), s32[]{:S(2)}) async-start(), calls=%async_computation.5 | async-start | bytes 294912 | tf_op jit(solution)/shard_map/reduce_scatter | solution.py:146
Sparse Core Ops, SparseCore 0:
  96.7 91.8 all-reduce.2
  630.5 76.1 reduce-scatter.1
